TPU v7x, 32 devices: a whole 2x2x4 slice. The times are simulated.
32 devices in a mesh: row: 8 (over y, x, core), col: 4 (over z).
Axes of the slice: x: 2, y: 2, z: 4, core: 2. Of those that a mesh axis runs over, the one named last changes fastest.
Arguments:
- teacher: bfloat16 [37, 1024, 1024], P(None, 'row', 'col'), may hold values from -320 to 320
- features: bfloat16 [64, 1024, 1024], P(None, 'row', 'col'), may hold values from -6 to 6
- valid: int32 [1024], replicated, may hold values from 0 to 1
- w_conv: bfloat16 [64, 64, 3, 3], replicated, may hold values from -0.25 to 0.25
- b_conv: float32 [64], replicated, may hold values from -3 to 3
- w_head: bfloat16 [37, 64], replicated, may hold values from -42 to 42
- b_head: float32 [37], replicated, may hold values from -4 to 4
Outputs:
- pair_loss: float32 [1024, 1024], P('row', 'col')
- loss: float32 [], replicated
- grad_conv: float32 [64, 64, 3, 3], replicated
- grad_conv_bias: float32 [64], replicated
- grad_head: float32 [37, 64], replicated
- grad_head_bias: float32 [37], replicated
All inputs are finite; a program needn't handle non-finite values.
Results may differ from a plain program's by a relative error of at most 0.004.
Values may be sent and summed in bfloat16 or wider, within the bound.
A program may use at most 192 MiB of HBM per device.

v0:
```python
import functools

import jax
import jax.numpy as jnp
from jax import lax
from jax.experimental import pallas as pl
from jax.experimental.pallas import tpu as pltpu
from jax.sharding import PartitionSpec as P

STEP = 4
VMEM_BYTES = 60 * 1024 * 1024


def shift_in(cells, axis, dim):
    count = lax.axis_size(axis)
    head = lax.slice_in_dim(cells, 0, STEP, axis=dim)
    tail = lax.slice_in_dim(cells, cells.shape[dim] - STEP, cells.shape[dim], axis=dim)
    before = lax.ppermute(tail, axis, [(i, i + 1) for i in range(count - 1)])
    after = lax.ppermute(head, axis, [(i + 1, i) for i in range(count - 1)])
    return before, after


def conv_kernel(rows, cols, ch, own_ref, top_ref, bottom_ref, side_ref, w_ref, b_ref, wide_ref, pre_ref):
    group = (rows + 2 * STEP) // STEP
    span = 3 * ch
    lane = lax.broadcasted_iota(jnp.int32, (ch, cols), 1)

    def widen(at, row):
        side = side_ref[at].astype(jnp.float32)
        side = jnp.concatenate([side] * (cols // 128), axis=1)
        middle = row.astype(jnp.float32)
        left = jnp.where(lane < STEP, side, pltpu.roll(middle, STEP, 1))
        right = jnp.where(lane >= cols - STEP, side, pltpu.roll(middle, cols - STEP, 1))
        start = pl.multiple_of(((at % STEP) * group + at // STEP) * span, span)
        wide_ref[pl.ds(start, ch), :] = left.astype(jnp.bfloat16)
        wide_ref[pl.ds(start + ch, ch), :] = row
        wide_ref[pl.ds(start + 2 * ch, ch), :] = right.astype(jnp.bfloat16)

    for i in range(STEP):
        widen(i, top_ref[i])
        widen(rows + STEP + i, bottom_ref[i])

    @pl.loop(0, rows, unroll=4)
    def _(y):
        widen(y + STEP, own_ref[y])

    bias = jnp.broadcast_to(b_ref[...], (ch, cols))

    @pl.loop(0, rows, unroll=4)
    def _(y):
        start = pl.multiple_of(((y % STEP) * group + y // STEP) * span, span)
        window = wide_ref[pl.ds(start, 3 * span), :]
        pre_ref[y] = jnp.dot(w_ref[...], window, preferred_element_type=jnp.float32) + bias


def rest_kernel(
    block, rows, cols, ch, bins, total,
    rv_ref, cv_ref, pre_ref, own_ref, mirror_ref, wide_ref, wh_ref, wht_ref, bh_ref,
    pair_ref, sums_ref, gw_acc, gh_acc, hb_acc, cb_acc, loss_acc,
):
    group = (rows + 2 * STEP) // STEP
    span = 3 * ch
    step = pl.program_id(0)

    @pl.when(step == 0)
    def _():
        for acc in (gw_acc, gh_acc, hb_acc, cb_acc, loss_acc):
            acc[...] = jnp.zeros_like(acc)

    bias = jnp.broadcast_to(bh_ref[...], (bins, cols))

    @pl.loop(0, block, unroll=4)
    def _(i):
        y = step * block + i
        pre = pre_ref[i]
        slope = jnp.exp(jnp.minimum(pre, 0.0))
        act = jnp.where(pre > 0, pre, slope - 1.0).astype(jnp.bfloat16)
        logits = jnp.dot(wh_ref[...], act, preferred_element_type=jnp.float32) + bias
        z = logits - jnp.max(logits, axis=0, keepdims=True)
        ez = jnp.exp(z)
        zs = jnp.sum(ez, axis=0, keepdims=True)
        logq = z - jnp.log(zs)
        sym = 0.5 * (own_ref[i].astype(jnp.float32) + mirror_ref[i].astype(jnp.float32))
        et = jnp.exp(sym - jnp.max(sym, axis=0, keepdims=True))
        target = et * (1.0 / jnp.sum(et, axis=0, keepdims=True))
        weight = rv_ref[y] * cv_ref[...]
        loss = -weight * jnp.sum(target * logq, axis=0, keepdims=True)
        pair_ref[pl.ds(i, 1), :] = loss
        loss_acc[...] += loss
        dlog = ((weight * (1.0 / total)) * (ez * (1.0 / zs) - target)).astype(jnp.bfloat16)
        hb_acc[...] += dlog.astype(jnp.float32)
        gh_acc[...] += lax.dot_general(dlog, act, (((1,), (1,)), ((), ())), preferred_element_type=jnp.float32)
        back = jnp.dot(wht_ref[...], dlog, preferred_element_type=jnp.float32)
        dpre = (back * slope).astype(jnp.bfloat16)
        cb_acc[...] += dpre.astype(jnp.float32)
        start = pl.multiple_of(((y % STEP) * group + y // STEP) * span, span)
        window = wide_ref[pl.ds(start, 3 * span), :]
        gw_acc[...] += lax.dot_general(window, dpre, (((1,), (1,)), ((), ())), preferred_element_type=jnp.float32)

    @pl.when(step == pl.num_programs(0) - 1)
    def _():
        half = 9 * ch // 2
        sums_ref[...] = jnp.zeros_like(sums_ref)
        sums_ref[0:half, 0:ch] = gw_acc[0:half, :]
        sums_ref[0:half, ch : 2 * ch] = gw_acc[half:, :]
        sums_ref[half : half + bins, 0:ch] = gh_acc[...]
        sums_ref[half : half + bins, ch : ch + 1] = jnp.sum(hb_acc[...], axis=1, keepdims=True)
        sums_ref[half + 40 : half + 40 + ch, 0:1] = jnp.sum(cb_acc[...], axis=1, keepdims=True)
        sums_ref[half + 40 : half + 41, 1:2] = jnp.sum(loss_acc[...], axis=1, keepdims=True)


def sum_kernel(n_row, n_col, chunk, x_ref, out_ref, row_slots, part, col_slots, gathered, rs_send, rs_recv, col_send, col_recv, ag_send, ag_recv):
    row, col = lax.axis_index("row"), lax.axis_index("col")
    row_peers = [lax.rem(row + o, n_row) for o in range(1, n_row)]
    col_peers = [lax.rem(col + o, n_col) for o in range(1, n_col)]
    mesh_id = pl.DeviceIdType.MESH
    barrier = pltpu.get_barrier_semaphore()
    for peer in row_peers:
        pl.semaphore_signal(barrier, inc=1, device_id=(peer, col), device_id_type=mesh_id)
    for peer in col_peers:
        pl.semaphore_signal(barrier, inc=1, device_id=(row, peer), device_id_type=mesh_id)
    pl.semaphore_wait(barrier, n_row + n_col - 2)

    def piece(index):
        return pl.ds(pl.multiple_of(index * chunk, chunk), chunk)

    def send(src, dst, send_sem, recv_sem, device):
        copy = pltpu.make_async_remote_copy(
            src_ref=src, dst_ref=dst, send_sem=send_sem, recv_sem=recv_sem, device_id=device, device_id_type=mesh_id
        )
        copy.start()
        return copy

    copies = [
        send(x_ref.at[piece(peer)], row_slots.at[o], rs_send.at[o], rs_recv.at[o], (peer, col))
        for o, peer in enumerate(row_peers)
    ]
    total = x_ref[piece(row), :]
    for o, copy in enumerate(copies):
        copy.wait_recv()
        total = total + row_slots[o]
    part[...] = total
    col_slots[col] = total
    col_copies = [
        send(part, col_slots.at[col], col_send.at[o], col_recv.at[o], (row, peer)) for o, peer in enumerate(col_peers)
    ]
    for copy in copies:
        copy.wait_send()
    for copy in col_copies:
        copy.wait_recv()
    for copy in col_copies:
        copy.wait_send()
    total = col_slots[0]
    for c in range(1, n_col):
        total = total + col_slots[c]
    part[...] = total
    gathered[piece(row), :] = total
    copies = [
        send(part, gathered.at[piece(row)], ag_send.at[o], ag_recv.at[o], (peer, col)) for o, peer in enumerate(row_peers)
    ]
    for copy in copies:
        copy.wait_recv()
    for copy in copies:
        copy.wait_send()
    out_ref[...] = gathered[...]


def summed(x):
    n_row, n_col = lax.axis_size("row"), lax.axis_size("col")
    chunk = x.shape[0] // n_row
    lanes = x.shape[1]
    dma = pltpu.SemaphoreType.DMA
    return pl.pallas_call(
        functools.partial(sum_kernel, n_row, n_col, chunk),
        name="sum_over_devices",
        out_shape=jax.ShapeDtypeStruct(x.shape, x.dtype),
        in_specs=[pl.BlockSpec(memory_space=pltpu.VMEM)],
        out_specs=pl.BlockSpec(memory_space=pltpu.VMEM),
        scratch_shapes=[
            pltpu.VMEM((n_row - 1, chunk, lanes), x.dtype),
            pltpu.VMEM((chunk, lanes), x.dtype),
            pltpu.VMEM((n_col, chunk, lanes), x.dtype),
            pltpu.VMEM(x.shape, x.dtype),
            dma((n_row - 1,)), dma((n_row - 1,)),
            dma((n_col - 1,)), dma((n_col - 1,)),
            dma((n_row - 1,)), dma((n_row - 1,)),
        ],
        compiler_params=pltpu.CompilerParams(collective_id=0, has_side_effects=True),
    )(x)

def mirrored(teacher):
    bins, rows, cols = teacher.shape
    n_row, n_col = lax.axis_size("row"), lax.axis_size("col")
    k = n_row // n_col
    ways = 4
    core = lax.axis_index("row") % k
    strip = rows // ways
    got = [[None] * ways for _ in range(k)]
    places = [(p, u, z) for p in range(n_col) for u in range(k) for z in range(n_col)]
    at = lambda p, u, z: (p * k + u) * n_col + z
    strips = []
    for d in range(ways):
        q = lax.slice_in_dim(teacher, d * strip, (d + 1) * strip, axis=1)
        if d:
            q = lax.ppermute(q, ("row", "col"), [(at(p, u, z), at(p ^ d, u, z)) for p, u, z in places])
        strips.append(q)
    for d, q in enumerate(strips):
        for e in range(k):
            half = (core + e) % k
            piece = lax.dynamic_slice_in_dim(q, half * rows, rows, 2) if k > 1 else q
            moves = [(at(p, u, z), at(z, (u + e) % k, p ^ d)) for p, u, z in places]
            got[e][d] = lax.ppermute(piece, ("row", "col"), moves)
    parts = [jnp.concatenate(g, axis=1) for g in got]
    if k == 1:
        return parts[0]
    stacked = jnp.stack(parts)
    return jnp.concatenate(
        [lax.dynamic_index_in_dim(stacked, (core - j) % k, 0, False) for j in range(k)], axis=1
    )


def on_device(teacher, features, valid, w_conv, b_conv, w_head, b_head):
    bins, rows, cols = teacher.shape
    ch = features.shape[0]
    n_row, n_col = lax.axis_size("row"), lax.axis_size("col")
    total = rows * n_row
    row_me, col_me = lax.axis_index("row"), lax.axis_index("col")

    feat = jnp.transpose(features, (1, 0, 2))
    top, bottom = shift_in(feat, "row", 0)
    edge = jnp.concatenate(
        [
            jnp.concatenate([top[:, :, :STEP], feat[:, :, :STEP], bottom[:, :, :STEP]], axis=0),
            jnp.concatenate([top[:, :, -STEP:], feat[:, :, -STEP:], bottom[:, :, -STEP:]], axis=0),
        ],
        axis=2,
    )
    left = lax.ppermute(edge[:, :, STEP:], "col", [(i, i + 1) for i in range(n_col - 1)])
    right = lax.ppermute(edge[:, :, :STEP], "col", [(i + 1, i) for i in range(n_col - 1)])
    side = jnp.concatenate([left, jnp.zeros((rows + 2 * STEP, ch, 128 - 2 * STEP), left.dtype), right], axis=2)

    mirror = mirrored(teacher)

    kernel_w = jnp.transpose(w_conv, (0, 2, 3, 1)).reshape(ch, 9 * ch)
    wide, pre = pl.pallas_call(
        functools.partial(conv_kernel, rows, cols, ch),
        name="conv_forward",
        out_shape=(
            jax.ShapeDtypeStruct(((rows + 2 * STEP) * 3 * ch, cols), jnp.bfloat16),
            jax.ShapeDtypeStruct((rows, ch, cols), jnp.float32),
        ),
        in_specs=[pl.BlockSpec(memory_space=pltpu.VMEM)] * 6,
        out_specs=(pl.BlockSpec(memory_space=pltpu.VMEM),) * 2,
        compiler_params=pltpu.CompilerParams(vmem_limit_bytes=VMEM_BYTES),
        cost_estimate=pl.CostEstimate(
            flops=2 * 9 * ch * ch * rows * cols, bytes_accessed=30_000_000, transcendentals=0
        ),
    )(feat, top, bottom, side, kernel_w, b_conv[:, None])

    mirror = jnp.transpose(mirror, (2, 0, 1))
    own = jnp.transpose(teacher, (1, 0, 2))

    valid_f = valid.astype(jnp.float32)
    count = jnp.sum(valid_f) ** 2
    row_valid = lax.dynamic_slice_in_dim(valid_f, row_me * rows, rows, 0)
    col_valid = lax.dynamic_slice_in_dim(valid_f, col_me * cols, cols, 0)

    block = 8
    half = 9 * ch // 2
    height = half + 40 + ch
    height = -(-height // (8 * n_row)) * 8 * n_row
    whole = lambda *shape: pl.BlockSpec(shape, lambda g: (0,) * len(shape), pipeline_mode=pl.Buffered(1))
    pair_loss, sums = pl.pallas_call(
        functools.partial(rest_kernel, block, rows, cols, ch, bins, total),
        name="loss_and_grads",
        grid=(rows // block,),
        out_shape=(
            jax.ShapeDtypeStruct((rows, cols), jnp.float32),
            jax.ShapeDtypeStruct((height, 2 * ch), jnp.float32),
        ),
        in_specs=[
            pl.BlockSpec(memory_space=pltpu.SMEM),
            whole(1, cols),
            pl.BlockSpec((block, ch, cols), lambda g: (g, 0, 0)),
            pl.BlockSpec((block, bins, cols), lambda g: (g, 0, 0)),
            pl.BlockSpec((block, bins, cols), lambda g: (g, 0, 0)),
            whole((rows + 2 * STEP) * 3 * ch, cols),
            whole(bins, ch),
            whole(ch, bins),
            whole(bins, 1),
        ],
        out_specs=(
            pl.BlockSpec((block, cols), lambda g: (g, 0)),
            pl.BlockSpec((height, 2 * ch), lambda g: (0, 0)),
        ),
        scratch_shapes=[
            pltpu.VMEM((9 * ch, ch), jnp.float32),
            pltpu.VMEM((bins, ch), jnp.float32),
            pltpu.VMEM((bins, cols), jnp.float32),
            pltpu.VMEM((ch, cols), jnp.float32),
            pltpu.VMEM((1, cols), jnp.float32),
        ],
        compiler_params=pltpu.CompilerParams(
            vmem_limit_bytes=VMEM_BYTES, dimension_semantics=("arbitrary",)
        ),
    )(row_valid, col_valid[None, :], pre, own, mirror, wide, w_head, w_head.T, b_head[:, None])

    sums = summed(sums)
    grad = jnp.concatenate([sums[:half, :ch], sums[:half, ch:]], axis=0)
    grad_cv = jnp.transpose(grad.reshape(3, 3, ch, ch), (3, 2, 0, 1))
    grad_hd = sums[half : half + bins, :ch]
    grad_hb = sums[half : half + bins, ch]
    grad_cb = sums[half + 40 : half + 40 + ch, 0]
    loss = sums[half + 40, 1] / count
    return (pair_loss, loss, grad_cv, grad_cb, grad_hd, grad_hb)


def solution(mesh):
    in_specs = (P(None, "row", "col"), P(None, "row", "col"), P(), P(), P(), P(), P())
    out_specs = (P("row", "col"), P(), P(), P(), P(), P())
    return jax.shard_map(
        on_device, mesh=mesh, in_specs=in_specs, out_specs=out_specs, check_vma=False
    )
```

profile of v0, /device:TPU:0, one launch (start us, length us, event | category | flops | bytes accessed | tf_op | source)
XLA Modules:
  0.0 232.7 jit_solution(14280921393641057948)
XLA Ops:
  0.6 4.7 %copy.52 = bf16[64,128,256]{2,0,1:T(8,128)(2,1)S(1)} copy(bf16[64,128,256]{2,1,0:T(8,128)(2,1)} %param.8) | data formatting | bytes 8388608 | tf_op args[1]
  5.4 2.4 %collective-permute-start = (bf16[4,64,256]{2,1,0:T(8,128)(2,1)S(1)}, bf16[4,64,256]{2,1,0:T(8,128)(2,1)S(1)}, u32[]{:S(2)}, u32[]{:S(2)}) collective-permute-start(bf16[4,64,256]{2,1,0:T(8,128)(2,1)S(1)} %get-tuple-element.17), channel_id=1, source_target_pairs={{0,4},{4,8},{8,12},{12,16},{16,20},{20,24},{24,28},{1,5},{5,9},{9,... | collective-permute-start | bytes 393224 | tf_op jit(solution)/shard_map/ppermute | solution.py:18
  10.3 5.8 %collective-permute-start.9 = (bf16[37,32,256]{2,1,0:T(8,128)(2,1)}, bf16[37,32,256]{2,1,0:T(8,128)(2,1)}, u32[]{:S(2)}, u32[]{:S(2)}) collective-permute-start(bf16[37,32,256]{2,1,0:T(8,128)(2,1)} %get-tuple-element.22), channel_id=1, source_target_pairs={{0,24},{1,25},{2,26},{3,27},{4,28},{5,29},{6,30},{7,31},{8,16},{9,... | collective-permute-start | bytes 1818632 | tf_op jit(solution)/shard_map/ppermute | solution.py:205
  17.6 3.1 %fusion.2 = (bf16[128,64,4]{2,1,0:T(8,128)(2,1)}, bf16[128,64,4]{2,1,0:T(8,128)(2,1)}) fusion(bf16[128,64,256]{2,1,0:T(8,128)(2,1)S(1)} %bitcast.24), kind=kLoop, calls=%fused_computation.26 | loop fusion | bytes 262144 | tf_op jit(solution)/shard_map/slice | solution.py:234
  20.6 2.8 %copy.53 = bf16[37,128,256]{2,0,1:T(8,128)(2,1)} copy(bf16[37,128,256]{2,1,0:T(8,128)(2,1)S(1)} %copy-done.1) | data formatting | bytes 4849664 | tf_op args[0]
  25.5 3.8 %copy.37 = bf16[128,64,4]{0,1,2:T(8,128)(2,1)S(1)} copy(bf16[128,64,4]{2,1,0:T(8,128)(2,1)} %get-tuple-element.15) | data formatting | bytes 131072 | tf_op jit(solution)/shard_map/slice | solution.py:233
  29.3 2.2 copy.34
  41.2 4.6 %collective-permute-start.2 = (bf16[136,64,4]{0,1,2:T(8,128)(2,1)S(1)}, bf16[136,64,4]{0,1,2:T(8,128)(2,1)S(1)}, u32[]{:S(2)}, u32[]{:S(2)}) collective-permute-start(bf16[136,64,4]{0,1,2:T(8,128)(2,1)S(1)} %pad_maximum_fusion.2), channel_id=1, source_target_pairs={{0,1},{1,2},{2,3},{4,5},{5,6},{6,7},{8,9},{9,10},{10,11},{12,13},{... | collective-permute-start | bytes 208904 | tf_op jit(solution)/shard_map/ppermute | solution.py:238
  46.6 1.6 collective-permute-start.4
  48.2 3.6 %copy.40 = bf16[136,64,4]{2,1,0:T(8,128)(2,1)S(1)} copy(bf16[136,64,4]{0,1,2:T(8,128)(2,1)S(1)} %collective-permute-done.3) | data formatting | bytes 139264 | tf_op jit(solution)/shard_map/ppermute | solution.py:239
  51.9 4.4 %copy.39 = bf16[136,64,4]{2,1,0:T(8,128)(2,1)} copy(bf16[136,64,4]{0,1,2:T(8,128)(2,1)S(1)} %collective-permute-done.2) | data formatting | bytes 139264 | tf_op jit(solution)/shard_map/ppermute | solution.py:238
  57.5 5.9 %collective-permute-start.10 = (bf16[37,32,128]{2,1,0:T(8,128)(2,1)S(1)}, bf16[37,32,128]{2,1,0:T(8,128)(2,1)S(1)}, u32[]{:S(2)}, u32[]{:S(2)}) collective-permute-start(bf16[37,32,128]{2,1,0:T(8,128)(2,1)S(1)} %get-tuple-element.31), channel_id=1, source_target_pairs={{0,3},{1,11},{2,19},{3,27},{4,7},{5,15},{6,23},{7,31},{8,2},{9,10}... | collective-permute-start | bytes 909320 | tf_op jit(solution)/shard_map/ppermute | solution.py:212
  65.3 1.9 constant_dynamic-slice_fusion.2
  67.3 2.8 %pad_maximum_fusion.side_ref = bf16[136,64,128]{2,1,0:T(8,128)(2,1)} fusion(bf16[136,64,4]{2,1,0:T(8,128)(2,1)S(1)} %copy.40, bf16[136,64,4]{2,1,0:T(8,128)(2,1)S(1)} %copy-done.2, bf16[128]{0:T(256)(128)(2,1)S(1)} %copy-done.15), kind=kLoop, calls=%fused_computation.7 | loop fusion | flops 6684672 | bytes 2367744 | tf_op jit(solution)/shard_map/concatenate | solution.py:240
  70.1 23.4 %collective-permute-start.14 = (bf16[37,32,128]{2,1,0:T(8,128)(2,1)S(1)}, bf16[37,32,128]{2,1,0:T(8,128)(2,1)S(1)}, u32[]{:S(2)}, u32[]{:S(2)}) collective-permute-start(bf16[37,32,128]{2,1,0:T(8,128)(2,1)S(1)} %get-tuple-element.30), channel_id=1, source_target_pairs={{0,7},{1,15},{2,23},{3,31},{4,3},{5,11},{6,19},{7,27},{8,6},{9,14}... | collective-permute-start | bytes 909320 | tf_op jit(solution)/shard_map/ppermute | solution.py:212
  95.4 26.1 %conv_forward.1 = (bf16[26112,256]{1,0:T(8,128)(2,1)}, f32[128,64,256]{2,1,0:T(8,128)}) custom-call(bf16[128,64,256]{2,1,0:T(8,128)(2,1)} %bitcast.25, bf16[4,64,256]{2,1,0:T(8,128)(2,1)} %copy-done.9, bf16[4,64,256]{2,1,0:T(8,128)(2,1)} %copy-done.10, bf16[136,64,128]{2,1,0:T(8,128)(2,1)} %pad_maximum_fusion.side_ref, bf16[64,576]{1,0:T(8,128)(2,1)} %copy.42.w_ref, ...), custom_call_target="tpu_custom_call" | custom-call | flops 2415919104 | bytes 30000000 | tf_op jit(solution)/shard_map/conv_forward/pallas_call | solution.py:245
  122.8 1.9 fusion.1
  124.8 1.4 copy.46
  126.1 2.1 copy.45
  128.3 1.8 maximum_bitcast_fusion.mirror_ref
  130.1 49.0 %loss_and_grads.1 = (f32[128,256]{1,0:T(8,128)}, f32[448,128]{1,0:T(8,128)}) custom-call(f32[128]{0:T(128)} %dynamic_slice.37.rv_ref, f32[1,256]{1,0:T(1,128)} %bitcast.34, f32[128,64,256]{2,1,0:T(8,128)} %get-tuple-element.10.pre_ref, bf16[128,37,256]{2,1,0:T(8,128)(2,1)} %bitcast.26, bf16[128,37,256]{2,1,0:T(8,128)(2,1)} %maximum_bitcast_fusion.mirror_ref, ...), custom_call_target="tpu_custom_call" | custom-call | tf_op jit(solution)/shard_map/loss_and_grads/pallas_call | solution.py:273
  179.1 44.4 %sum_over_devices.1 = f32[448,128]{1,0:T(8,128)} custom-call(f32[448,128]{1,0:T(8,128)} %get-tuple-element.13.x_ref), custom_call_target="tpu_custom_call" | custom-call | tf_op jit(solution)/shard_map/sum_over_devices/pallas_call | solution.py:173
  225.8 1.4 slice_reduce_fusion
  228.6 1.4 slice_reduce_fusion.1
  (87 shorter events, 26.2 us)
Async XLA Ops:
  0.6 8.4 %copy-start.1 = (bf16[37,128,256]{2,1,0:T(8,128)(2,1)S(1)}, bf16[37,128,256]{2,1,0:T(8,128)(2,1)}, u32[]{:S(2)}) copy-start(bf16[37,128,256]{2,1,0:T(8,128)(2,1)} %param.7) | copy-start | bytes 7274500
  5.4 12.2 %copy-start = (bf16[64,128,256]{2,0,1:T(8,128)(2,1)}, bf16[64,128,256]{2,0,1:T(8,128)(2,1)S(1)}, u32[]{:S(2)}) copy-start(bf16[64,128,256]{2,0,1:T(8,128)(2,1)S(1)} %copy.52) | copy-start | bytes 12582916
  5.4 32.3 %collective-permute-start = (bf16[4,64,256]{2,1,0:T(8,128)(2,1)S(1)}, bf16[4,64,256]{2,1,0:T(8,128)(2,1)S(1)}, u32[]{:S(2)}, u32[]{:S(2)}) collective-permute-start(bf16[4,64,256]{2,1,0:T(8,128)(2,1)S(1)} %get-tuple-element.17), channel_id=1, source_target_pairs={{0,4},{4,8},{8,12},{12,16},{16,20},{20,24},{24,28},{1,5},{5,9},{9,... | collective-permute-start | bytes 393224 | tf_op jit(solution)/shard_map/ppermute | solution.py:18
  7.8 29.3 %collective-permute-start.1 = (bf16[4,64,256]{2,1,0:T(8,128)(2,1)S(1)}, bf16[4,64,256]{2,1,0:T(8,128)(2,1)S(1)}, u32[]{:S(2)}, u32[]{:S(2)}) collective-permute-start(bf16[4,64,256]{2,1,0:T(8,128)(2,1)S(1)} %get-tuple-element.16), channel_id=1, source_target_pairs={{4,0},{8,4},{12,8},{16,12},{20,16},{24,20},{28,24},{5,1},{9,5},{13... | collective-permute-start | bytes 393224 | tf_op jit(solution)/shard_map/ppermute | solution.py:19
  10.3 45.9 %collective-permute-start.9 = (bf16[37,32,256]{2,1,0:T(8,128)(2,1)}, bf16[37,32,256]{2,1,0:T(8,128)(2,1)}, u32[]{:S(2)}, u32[]{:S(2)}) collective-permute-start(bf16[37,32,256]{2,1,0:T(8,128)(2,1)} %get-tuple-element.22), channel_id=1, source_target_pairs={{0,24},{1,25},{2,26},{3,27},{4,28},{5,29},{6,30},{7,31},{8,16},{9,... | collective-permute-start | bytes 1818632 | tf_op jit(solution)/shard_map/ppermute | solution.py:205
  16.1 47.2 %collective-permute-start.7 = (bf16[37,32,256]{2,1,0:T(8,128)(2,1)}, bf16[37,32,256]{2,1,0:T(8,128)(2,1)}, u32[]{:S(2)}, u32[]{:S(2)}) collective-permute-start(bf16[37,32,256]{2,1,0:T(8,128)(2,1)} %get-tuple-element.23), channel_id=1, source_target_pairs={{0,16},{1,17},{2,18},{3,19},{4,20},{5,21},{6,22},{7,23},{8,24},{9,... | collective-permute-start | bytes 1818632 | tf_op jit(solution)/shard_map/ppermute | solution.py:205
  16.7 48.7 %collective-permute-start.5 = (bf16[37,32,256]{2,1,0:T(8,128)(2,1)}, bf16[37,32,256]{2,1,0:T(8,128)(2,1)}, u32[]{:S(2)}, u32[]{:S(2)}) collective-permute-start(bf16[37,32,256]{2,1,0:T(8,128)(2,1)} %get-tuple-element.21), channel_id=1, source_target_pairs={{0,8},{1,9},{2,10},{3,11},{4,12},{5,13},{6,14},{7,15},{8,0},{9,1},... | collective-permute-start | bytes 1818632 | tf_op jit(solution)/shard_map/ppermute | solution.py:205
  23.5 8.0 %copy-start.8 = (bf16[64,64,3,3]{1,0,3,2:T(8,128)(2,1)S(1)}, bf16[64,64,3,3]{1,0,3,2:T(8,128)(2,1)}, u32[]{:S(2)}) copy-start(bf16[64,64,3,3]{1,0,3,2:T(8,128)(2,1)} %param.10) | copy-start | bytes 221188
  25.5 8.3 %copy-start.14 = (f32[37]{0:T(128)S(1)}, f32[37]{0:T(128)}, u32[]{:S(2)}) copy-start(f32[37]{0:T(128)} %param.13) | copy-start | bytes 448
  25.5 9.0 %copy-start.12 = (s32[1024]{0:T(1024)S(1)}, s32[1024]{0:T(1024)}, u32[]{:S(2)}) copy-start(s32[1024]{0:T(1024)} %param.9) | copy-start | bytes 12292
  38.6 8.0 %collective-permute-start.3 = (bf16[136,64,4]{0,1,2:T(8,128)(2,1)S(1)}, bf16[136,64,4]{0,1,2:T(8,128)(2,1)S(1)}, u32[]{:S(2)}, u32[]{:S(2)}) collective-permute-start(bf16[136,64,4]{0,1,2:T(8,128)(2,1)S(1)} %pad_maximum_fusion.3), channel_id=1, source_target_pairs={{1,0},{2,1},{3,2},{5,4},{6,5},{7,6},{9,8},{10,9},{11,10},{13,12},{... | collective-permute-start | bytes 208904 | tf_op jit(solution)/shard_map/ppermute | solution.py:239
  41.2 10.6 %collective-permute-start.2 = (bf16[136,64,4]{0,1,2:T(8,128)(2,1)S(1)}, bf16[136,64,4]{0,1,2:T(8,128)(2,1)S(1)}, u32[]{:S(2)}, u32[]{:S(2)}) collective-permute-start(bf16[136,64,4]{0,1,2:T(8,128)(2,1)S(1)} %pad_maximum_fusion.2), channel_id=1, source_target_pairs={{0,1},{1,2},{2,3},{4,5},{5,6},{6,7},{8,9},{9,10},{10,11},{12,13},{... | collective-permute-start | bytes 208904 | tf_op jit(solution)/shard_map/ppermute | solution.py:238
  46.6 23.5 %collective-permute-start.4 = (bf16[37,32,128]{2,1,0:T(8,128)(2,1)}, bf16[37,32,128]{2,1,0:T(8,128)(2,1)S(1)}, u32[]{:S(2)}, u32[]{:S(2)}) collective-permute-start(bf16[37,32,128]{2,1,0:T(8,128)(2,1)} %get-tuple-element.25), channel_id=1, source_target_pairs={{0,0},{1,8},{2,16},{3,24},{4,4},{5,12},{6,20},{7,28},{8,1},{9,9},{... | collective-permute-start | bytes 909320 | tf_op jit(solution)/shard_map/ppermute | solution.py:212
  51.8 15.5 %copy-start.15 = (bf16[128]{0:T(256)(128)(2,1)S(1)}, bf16[128]{0:T(256)(128)(2,1)}, u32[]{:S(2)}) copy-start(bf16[128]{0:T(256)(128)(2,1)} %pad.15.clone) | copy-start | bytes 772
  51.8 70.8 %collective-permute-start.11 = (bf16[37,32,128]{2,1,0:T(8,128)(2,1)S(1)}, bf16[37,32,128]{2,1,0:T(8,128)(2,1)S(1)}, u32[]{:S(2)}, u32[]{:S(2)}) collective-permute-start(bf16[37,32,128]{2,1,0:T(8,128)(2,1)S(1)} %get-tuple-element.24), channel_id=1, source_target_pairs={{0,4},{1,12},{2,20},{3,28},{4,0},{5,8},{6,16},{7,24},{8,5},{9,13},... | collective-permute-start | bytes 909320 | tf_op jit(solution)/shard_map/ppermute | solution.py:212
  56.3 11.0 %copy-start.2 = (bf16[136,64,4]{2,1,0:T(8,128)(2,1)S(1)}, bf16[136,64,4]{2,1,0:T(8,128)(2,1)}, u32[]{:S(2)}) copy-start(bf16[136,64,4]{2,1,0:T(8,128)(2,1)} %copy.39) | copy-start | bytes 208900
  57.5 36.0 %collective-permute-start.10 = (bf16[37,32,128]{2,1,0:T(8,128)(2,1)S(1)}, bf16[37,32,128]{2,1,0:T(8,128)(2,1)S(1)}, u32[]{:S(2)}, u32[]{:S(2)}) collective-permute-start(bf16[37,32,128]{2,1,0:T(8,128)(2,1)S(1)} %get-tuple-element.31), channel_id=1, source_target_pairs={{0,3},{1,11},{2,19},{3,27},{4,7},{5,15},{6,23},{7,31},{8,2},{9,10}... | collective-permute-start | bytes 909320 | tf_op jit(solution)/shard_map/ppermute | solution.py:212
  64.5 29.7 %collective-permute-start.8 = (bf16[37,32,128]{2,1,0:T(8,128)(2,1)S(1)}, bf16[37,32,128]{2,1,0:T(8,128)(2,1)S(1)}, u32[]{:S(2)}, u32[]{:S(2)}) collective-permute-start(bf16[37,32,128]{2,1,0:T(8,128)(2,1)S(1)} %get-tuple-element.29), channel_id=1, source_target_pairs={{0,2},{1,10},{2,18},{3,26},{4,6},{5,14},{6,22},{7,30},{8,3},{9,11}... | collective-permute-start | bytes 909320 | tf_op jit(solution)/shard_map/ppermute | solution.py:212
  67.3 54.2 %collective-permute-start.6 = (bf16[37,32,128]{2,1,0:T(8,128)(2,1)}, bf16[37,32,128]{2,1,0:T(8,128)(2,1)}, u32[]{:S(2)}, u32[]{:S(2)}) collective-permute-start(bf16[37,32,128]{2,1,0:T(8,128)(2,1)} %get-tuple-element.27), channel_id=1, source_target_pairs={{0,1},{1,9},{2,17},{3,25},{4,5},{5,13},{6,21},{7,29},{8,0},{9,8},{... | collective-permute-start | bytes 909320 | tf_op jit(solution)/shard_map/ppermute | solution.py:212
  70.1 52.6 %collective-permute-start.14 = (bf16[37,32,128]{2,1,0:T(8,128)(2,1)S(1)}, bf16[37,32,128]{2,1,0:T(8,128)(2,1)S(1)}, u32[]{:S(2)}, u32[]{:S(2)}) collective-permute-start(bf16[37,32,128]{2,1,0:T(8,128)(2,1)S(1)} %get-tuple-element.30), channel_id=1, source_target_pairs={{0,7},{1,15},{2,23},{3,31},{4,3},{5,11},{6,19},{7,27},{8,6},{9,14}... | collective-permute-start | bytes 909320 | tf_op jit(solution)/shard_map/ppermute | solution.py:212
  93.5 29.2 %collective-permute-start.13 = (bf16[37,32,128]{2,1,0:T(8,128)(2,1)S(1)}, bf16[37,32,128]{2,1,0:T(8,128)(2,1)S(1)}, u32[]{:S(2)}, u32[]{:S(2)}) collective-permute-start(bf16[37,32,128]{2,1,0:T(8,128)(2,1)S(1)} %get-tuple-element.28), channel_id=1, source_target_pairs={{0,6},{1,14},{2,22},{3,30},{4,2},{5,10},{6,18},{7,26},{8,7},{9,15}... | collective-permute-start | bytes 909320 | tf_op jit(solution)/shard_map/ppermute | solution.py:212
  94.9 26.6 %copy-start.5 = (bf16[37,32,128]{2,1,0:T(8,128)(2,1)S(1)}, bf16[37,32,128]{2,1,0:T(8,128)(2,1)}, u32[]{:S(2)}) copy-start(bf16[37,32,128]{2,1,0:T(8,128)(2,1)} %copy-done.4) | copy-start | bytes 909316
  94.9 26.6 %copy-start.7 = (bf16[37,32,128]{2,1,0:T(8,128)(2,1)S(1)}, bf16[37,32,128]{2,1,0:T(8,128)(2,1)}, u32[]{:S(2)}) copy-start(bf16[37,32,128]{2,1,0:T(8,128)(2,1)} %copy-done.6) | copy-start | bytes 909316
  94.9 27.7 %collective-permute-start.12 = (bf16[37,32,128]{2,1,0:T(8,128)(2,1)}, bf16[37,32,128]{2,1,0:T(8,128)(2,1)S(1)}, u32[]{:S(2)}, u32[]{:S(2)}) collective-permute-start(bf16[37,32,128]{2,1,0:T(8,128)(2,1)} %get-tuple-element.26), channel_id=1, source_target_pairs={{0,5},{1,13},{2,21},{3,29},{4,1},{5,9},{6,17},{7,25},{8,4},{9,12},... | collective-permute-start | bytes 909320 | tf_op jit(solution)/shard_map/ppermute | solution.py:212
  (7 other events, 29.2 us)
where the time goes:
time: 233 us
  Pallas kernels  120 us (52%)
  local copies, waits for them, and re-layouts  50.1 us (22%)
  starting transfers between devices  49.5 us (21%)
  other arithmetic  9.49 us (4%)
  between operations  4.07 us (2%)
    pallas_call x1, Pallas kernels, on_device(): pl.pallas_call(functools.partial(rest_kernel, block, rows, cols, ch, bins...  49 us
    pallas_call x1, Pallas kernels, summed(): pl.pallas_call(functools.partial(sum_kernel, n_row, n_col, chunk), name='...  44.4 us
    ppermute x8, starting transfers between devices, mirrored(): got[e][d] = lax.ppermute(piece, ('row', 'col'), moves)  32.7 us
    pallas_call x1, Pallas kernels, on_device(): pl.pallas_call(functools.partial(conv_kernel, rows, cols, ch), name='conv...  26.1 us
    unnamed x35, local copies, waits for them, and re-layouts  9.25 us
    ppermute x3, starting transfers between devices, mirrored(): lax.ppermute(q, ('row', 'col'), [(at(p, u, z), at(p ^ d, u, z)) for p, u,...  7.24 us
    slice x2, local copies, waits for them, and re-layouts, on_device(): feat[:, :, -STEP:]  5.29 us
    dynamic_slice x4, local copies, waits for them, and re-layouts, mirrored(): piece = lax.dynamic_slice_in_dim(q, half * rows, rows, 2) if k > 1 else q  5.14 us
  transfers between devices with their start and end apart: 15, of which 0 were waited for; matrix products, arithmetic and copies ran while one was open for 17% of the time, Pallas kernels for 11%

commit v1 on v0

--- a/solution.py
+++ b/solution.py
@@ -54,7 +54,7 @@
 
 
 def rest_kernel(
-    block, rows, cols, ch, bins, total,
+    wave, block, rows, cols, ch, bins, total,
     rv_ref, cv_ref, pre_ref, own_ref, mirror_ref, wide_ref, wh_ref, wht_ref, bh_ref,
     pair_ref, sums_ref, gw_acc, gh_acc, hb_acc, cb_acc, loss_acc,
 ):
@@ -67,12 +67,16 @@
         for acc in (gw_acc, gh_acc, hb_acc, cb_acc, loss_acc):
             acc[...] = jnp.zeros_like(acc)
 
-    bias = jnp.broadcast_to(bh_ref[...], (bins, cols))
-
-    @pl.loop(0, block, unroll=4)
-    def _(i):
-        y = step * block + i
-        pre = pre_ref[i]
+    bias = jnp.broadcast_to(bh_ref[...], (bins, wave * cols))
+
+    def side_by_side(ref, base):
+        return jnp.concatenate([ref[base + r] for r in range(wave)], axis=1)
+
+    def folded(value):
+        return functools.reduce(jnp.add, [value[:, r * cols : (r + 1) * cols] for r in range(wave)])
+
+    def rows_at(base):
+        pre = side_by_side(pre_ref, base)
         slope = jnp.exp(jnp.minimum(pre, 0.0))
         act = jnp.where(pre > 0, pre, slope - 1.0).astype(jnp.bfloat16)
         logits = jnp.dot(wh_ref[...], act, preferred_element_type=jnp.float32) + bias
@@ -80,22 +84,34 @@
         ez = jnp.exp(z)
         zs = jnp.sum(ez, axis=0, keepdims=True)
         logq = z - jnp.log(zs)
-        sym = 0.5 * (own_ref[i].astype(jnp.float32) + mirror_ref[i].astype(jnp.float32))
+        sym = 0.5 * (
+            side_by_side(own_ref, base).astype(jnp.float32) + side_by_side(mirror_ref, base).astype(jnp.float32)
+        )
         et = jnp.exp(sym - jnp.max(sym, axis=0, keepdims=True))
         target = et * (1.0 / jnp.sum(et, axis=0, keepdims=True))
-        weight = rv_ref[y] * cv_ref[...]
+        y = step * block + base
+        weight = jnp.concatenate([rv_ref[y + r] * cv_ref[...] for r in range(wave)], axis=1)
         loss = -weight * jnp.sum(target * logq, axis=0, keepdims=True)
-        pair_ref[pl.ds(i, 1), :] = loss
-        loss_acc[...] += loss
+        for r in range(wave):
+            pair_ref[base + r : base + r + 1, :] = loss[:, r * cols : (r + 1) * cols]
+        loss_acc[...] += folded(loss)
         dlog = ((weight * (1.0 / total)) * (ez * (1.0 / zs) - target)).astype(jnp.bfloat16)
-        hb_acc[...] += dlog.astype(jnp.float32)
+        hb_acc[...] += folded(dlog.astype(jnp.float32))
         gh_acc[...] += lax.dot_general(dlog, act, (((1,), (1,)), ((), ())), preferred_element_type=jnp.float32)
         back = jnp.dot(wht_ref[...], dlog, preferred_element_type=jnp.float32)
         dpre = (back * slope).astype(jnp.bfloat16)
-        cb_acc[...] += dpre.astype(jnp.float32)
-        start = pl.multiple_of(((y % STEP) * group + y // STEP) * span, span)
-        window = wide_ref[pl.ds(start, 3 * span), :]
-        gw_acc[...] += lax.dot_general(window, dpre, (((1,), (1,)), ((), ())), preferred_element_type=jnp.float32)
+        cb_acc[...] += folded(dpre.astype(jnp.float32))
+        windows = []
+        for r in range(wave):
+            place = (base + r) % STEP * group + (step * block + base + r) // STEP
+            start = pl.multiple_of(place * span, span)
+            windows.append(wide_ref[pl.ds(start, 3 * span), :])
+        gw_acc[...] += lax.dot_general(
+            jnp.concatenate(windows, axis=1), dpre, (((1,), (1,)), ((), ())), preferred_element_type=jnp.float32
+        )
+
+    for base in range(0, block, wave):
+        rows_at(base)
 
     @pl.when(step == pl.num_programs(0) - 1)
     def _():
@@ -265,13 +281,13 @@
     row_valid = lax.dynamic_slice_in_dim(valid_f, row_me * rows, rows, 0)
     col_valid = lax.dynamic_slice_in_dim(valid_f, col_me * cols, cols, 0)
 
-    block = 8
+    block, wave = 16, 4
     half = 9 * ch // 2
     height = half + 40 + ch
     height = -(-height // (8 * n_row)) * 8 * n_row
     whole = lambda *shape: pl.BlockSpec(shape, lambda g: (0,) * len(shape), pipeline_mode=pl.Buffered(1))
     pair_loss, sums = pl.pallas_call(
-        functools.partial(rest_kernel, block, rows, cols, ch, bins, total),
+        functools.partial(rest_kernel, wave, block, rows, cols, ch, bins, total),
         name="loss_and_grads",
         grid=(rows // block,),
         out_shape=(

time: 233 us -> 216 us (0.927)
  Pallas kernels: 120 us -> 102 us
    pallas_call x1, Pallas kernels: 49 us -> 31.7 us  [on_device(): pl.pallas_call(functools.partial(rest_kernel, wave, block, rows, cols, ch...]
  transfers between devices with their start and end apart: 15 -> 15, of which waited for: 0 -> 0; matrix products, arithmetic and copies ran while one was open for 17% -> 18% of each run, Pallas kernels for 11% -> 12%
where the time goes in v1:
time: 216 us; the launch traced here: 215 us
  Pallas kernels  102 us (47%)
  local copies, waits for them, and re-layouts  50.1 us (23%)
  starting transfers between devices  49.5 us (23%)
  other arithmetic  9.49 us (4%)
  between operations  4.07 us (2%)
    pallas_call x1, Pallas kernels, summed(): pl.pallas_call(functools.partial(sum_kernel, n_row, n_col, chunk), name='...  44.4 us
    ppermute x8, starting transfers between devices, mirrored(): got[e][d] = lax.ppermute(piece, ('row', 'col'), moves)  32.7 us
    pallas_call x1, Pallas kernels, on_device(): pl.pallas_call(functools.partial(rest_kernel, wave, block, rows, cols, ch...  31.7 us
    pallas_call x1, Pallas kernels, on_device(): pl.pallas_call(functools.partial(conv_kernel, rows, cols, ch), name='conv...  26.1 us
    unnamed x35, local copies, waits for them, and re-layouts  9.25 us
    ppermute x3, starting transfers between devices, mirrored(): lax.ppermute(q, ('row', 'col'), [(at(p, u, z), at(p ^ d, u, z)) for p, u,...  7.24 us
    slice x2, local copies, waits for them, and re-layouts, on_device(): feat[:, :, -STEP:]  5.29 us
    dynamic_slice x4, local copies, waits for them, and re-layouts, mirrored(): piece = lax.dynamic_slice_in_dim(q, half * rows, rows, 2) if k > 1 else q  5.14 us
  transfers between devices with their start and end apart: 15, of which 0 were waited for; matrix products, arithmetic and copies ran while one was open for 18% of the time, Pallas kernels for 12%

profile of v1, /device:TPU:0, one launch (start us, length us, event | category | flops | bytes accessed | tf_op | source)
XLA Modules:
  0.0 215.3 jit_solution(18407371765242097515)
XLA Ops:
  0.6 4.7 %copy.52 = bf16[64,128,256]{2,0,1:T(8,128)(2,1)S(1)} copy(bf16[64,128,256]{2,1,0:T(8,128)(2,1)} %param.8) | data formatting | bytes 8388608 | tf_op args[1]
  5.4 2.4 %collective-permute-start = (bf16[4,64,256]{2,1,0:T(8,128)(2,1)S(1)}, bf16[4,64,256]{2,1,0:T(8,128)(2,1)S(1)}, u32[]{:S(2)}, u32[]{:S(2)}) collective-permute-start(bf16[4,64,256]{2,1,0:T(8,128)(2,1)S(1)} %get-tuple-element.17), channel_id=1, source_target_pairs={{0,4},{4,8},{8,12},{12,16},{16,20},{20,24},{24,28},{1,5},{5,9},{9,... | collective-permute-start | bytes 393224 | tf_op jit(solution)/shard_map/ppermute | solution.py:18
  10.3 5.8 %collective-permute-start.9 = (bf16[37,32,256]{2,1,0:T(8,128)(2,1)}, bf16[37,32,256]{2,1,0:T(8,128)(2,1)}, u32[]{:S(2)}, u32[]{:S(2)}) collective-permute-start(bf16[37,32,256]{2,1,0:T(8,128)(2,1)} %get-tuple-element.22), channel_id=1, source_target_pairs={{0,24},{1,25},{2,26},{3,27},{4,28},{5,29},{6,30},{7,31},{8,16},{9,... | collective-permute-start | bytes 1818632 | tf_op jit(solution)/shard_map/ppermute | solution.py:221
  17.6 3.1 %fusion.2 = (bf16[128,64,4]{2,1,0:T(8,128)(2,1)}, bf16[128,64,4]{2,1,0:T(8,128)(2,1)}) fusion(bf16[128,64,256]{2,1,0:T(8,128)(2,1)S(1)} %bitcast.24), kind=kLoop, calls=%fused_computation.26 | loop fusion | bytes 262144 | tf_op jit(solution)/shard_map/slice | solution.py:250
  20.6 2.8 %copy.53 = bf16[37,128,256]{2,0,1:T(8,128)(2,1)} copy(bf16[37,128,256]{2,1,0:T(8,128)(2,1)S(1)} %copy-done.1) | data formatting | bytes 4849664 | tf_op args[0]
  25.5 3.8 %copy.37 = bf16[128,64,4]{0,1,2:T(8,128)(2,1)S(1)} copy(bf16[128,64,4]{2,1,0:T(8,128)(2,1)} %get-tuple-element.15) | data formatting | bytes 131072 | tf_op jit(solution)/shard_map/slice | solution.py:249
  29.3 2.2 %copy.34 = bf16[128,64,4]{0,1,2:T(8,128)(2,1)S(1)} copy(bf16[128,64,4]{2,1,0:T(8,128)(2,1)S(1)} %copy-done.3) | data formatting | bytes 131072 | tf_op jit(solution)/shard_map/slice | solution.py:250
  41.2 4.6 %collective-permute-start.2 = (bf16[136,64,4]{0,1,2:T(8,128)(2,1)S(1)}, bf16[136,64,4]{0,1,2:T(8,128)(2,1)S(1)}, u32[]{:S(2)}, u32[]{:S(2)}) collective-permute-start(bf16[136,64,4]{0,1,2:T(8,128)(2,1)S(1)} %pad_maximum_fusion.2), channel_id=1, source_target_pairs={{0,1},{1,2},{2,3},{4,5},{5,6},{6,7},{8,9},{9,10},{10,11},{12,13},{... | collective-permute-start | bytes 208904 | tf_op jit(solution)/shard_map/ppermute | solution.py:254
  46.6 1.6 collective-permute-start.4
  48.2 3.6 %copy.40 = bf16[136,64,4]{2,1,0:T(8,128)(2,1)S(1)} copy(bf16[136,64,4]{0,1,2:T(8,128)(2,1)S(1)} %collective-permute-done.3) | data formatting | bytes 139264 | tf_op jit(solution)/shard_map/ppermute | solution.py:255
  51.9 4.4 %copy.39 = bf16[136,64,4]{2,1,0:T(8,128)(2,1)} copy(bf16[136,64,4]{0,1,2:T(8,128)(2,1)S(1)} %collective-permute-done.2) | data formatting | bytes 139264 | tf_op jit(solution)/shard_map/ppermute | solution.py:254
  57.5 5.9 %collective-permute-start.10 = (bf16[37,32,128]{2,1,0:T(8,128)(2,1)S(1)}, bf16[37,32,128]{2,1,0:T(8,128)(2,1)S(1)}, u32[]{:S(2)}, u32[]{:S(2)}) collective-permute-start(bf16[37,32,128]{2,1,0:T(8,128)(2,1)S(1)} %get-tuple-element.31), channel_id=1, source_target_pairs={{0,3},{1,11},{2,19},{3,27},{4,7},{5,15},{6,23},{7,31},{8,2},{9,10}... | collective-permute-start | bytes 909320 | tf_op jit(solution)/shard_map/ppermute | solution.py:228
  65.3 1.9 constant_dynamic-slice_fusion.2
  67.3 2.8 %pad_maximum_fusion.side_ref = bf16[136,64,128]{2,1,0:T(8,128)(2,1)} fusion(bf16[136,64,4]{2,1,0:T(8,128)(2,1)S(1)} %copy.40, bf16[136,64,4]{2,1,0:T(8,128)(2,1)S(1)} %copy-done.2, bf16[128]{0:T(256)(128)(2,1)S(1)} %copy-done.15), kind=kLoop, calls=%fused_computation.7 | loop fusion | flops 6684672 | bytes 2367744 | tf_op jit(solution)/shard_map/concatenate | solution.py:256
  70.1 23.4 %collective-permute-start.14 = (bf16[37,32,128]{2,1,0:T(8,128)(2,1)S(1)}, bf16[37,32,128]{2,1,0:T(8,128)(2,1)S(1)}, u32[]{:S(2)}, u32[]{:S(2)}) collective-permute-start(bf16[37,32,128]{2,1,0:T(8,128)(2,1)S(1)} %get-tuple-element.30), channel_id=1, source_target_pairs={{0,7},{1,15},{2,23},{3,31},{4,3},{5,11},{6,19},{7,27},{8,6},{9,14}... | collective-permute-start | bytes 909320 | tf_op jit(solution)/shard_map/ppermute | solution.py:228
  95.4 26.1 %conv_forward.1 = (bf16[26112,256]{1,0:T(8,128)(2,1)}, f32[128,64,256]{2,1,0:T(8,128)}) custom-call(bf16[128,64,256]{2,1,0:T(8,128)(2,1)} %bitcast.25, bf16[4,64,256]{2,1,0:T(8,128)(2,1)} %copy-done.9, bf16[4,64,256]{2,1,0:T(8,128)(2,1)} %copy-done.10, bf16[136,64,128]{2,1,0:T(8,128)(2,1)} %pad_maximum_fusion.side_ref, bf16[64,576]{1,0:T(8,128)(2,1)} %copy.42.w_ref, ...), custom_call_target="tpu_custom_call" | custom-call | flops 2415919104 | bytes 30000000 | tf_op jit(solution)/shard_map/conv_forward/pallas_call | solution.py:261
  122.8 1.9 fusion.1
  124.8 1.4 copy.46
  126.1 2.1 copy.45
  128.3 1.8 maximum_bitcast_fusion.mirror_ref
  130.1 31.7 %loss_and_grads.1 = (f32[128,256]{1,0:T(8,128)}, f32[448,128]{1,0:T(8,128)}) custom-call(f32[128]{0:T(128)} %dynamic_slice.37.rv_ref, f32[1,256]{1,0:T(1,128)} %bitcast.34, f32[128,64,256]{2,1,0:T(8,128)} %get-tuple-element.10.pre_ref, bf16[128,37,256]{2,1,0:T(8,128)(2,1)} %bitcast.26, bf16[128,37,256]{2,1,0:T(8,128)(2,1)} %maximum_bitcast_fusion.mirror_ref, ...), custom_call_target="tpu_custom_call" | custom-call | tf_op jit(solution)/shard_map/loss_and_grads/pallas_call | solution.py:289
  161.8 44.4 %sum_over_devices.1 = f32[448,128]{1,0:T(8,128)} custom-call(f32[448,128]{1,0:T(8,128)} %get-tuple-element.13.x_ref), custom_call_target="tpu_custom_call" | custom-call | tf_op jit(solution)/shard_map/sum_over_devices/pallas_call | solution.py:189
  208.5 1.4 slice_reduce_fusion
  211.2 1.4 slice_reduce_fusion.1
  (87 shorter events, 26.2 us)
Async XLA Ops:
  0.6 8.4 %copy-start.1 = (bf16[37,128,256]{2,1,0:T(8,128)(2,1)S(1)}, bf16[37,128,256]{2,1,0:T(8,128)(2,1)}, u32[]{:S(2)}) copy-start(bf16[37,128,256]{2,1,0:T(8,128)(2,1)} %param.7) | copy-start | bytes 7274500
  5.4 12.2 %copy-start = (bf16[64,128,256]{2,0,1:T(8,128)(2,1)}, bf16[64,128,256]{2,0,1:T(8,128)(2,1)S(1)}, u32[]{:S(2)}) copy-start(bf16[64,128,256]{2,0,1:T(8,128)(2,1)S(1)} %copy.52) | copy-start | bytes 12582916
  5.4 32.3 %collective-permute-start = (bf16[4,64,256]{2,1,0:T(8,128)(2,1)S(1)}, bf16[4,64,256]{2,1,0:T(8,128)(2,1)S(1)}, u32[]{:S(2)}, u32[]{:S(2)}) collective-permute-start(bf16[4,64,256]{2,1,0:T(8,128)(2,1)S(1)} %get-tuple-element.17), channel_id=1, source_target_pairs={{0,4},{4,8},{8,12},{12,16},{16,20},{20,24},{24,28},{1,5},{5,9},{9,... | collective-permute-start | bytes 393224 | tf_op jit(solution)/shard_map/ppermute | solution.py:18
  7.8 29.3 %collective-permute-start.1 = (bf16[4,64,256]{2,1,0:T(8,128)(2,1)S(1)}, bf16[4,64,256]{2,1,0:T(8,128)(2,1)S(1)}, u32[]{:S(2)}, u32[]{:S(2)}) collective-permute-start(bf16[4,64,256]{2,1,0:T(8,128)(2,1)S(1)} %get-tuple-element.16), channel_id=1, source_target_pairs={{4,0},{8,4},{12,8},{16,12},{20,16},{24,20},{28,24},{5,1},{9,5},{13... | collective-permute-start | bytes 393224 | tf_op jit(solution)/shard_map/ppermute | solution.py:19
  10.3 45.9 %collective-permute-start.9 = (bf16[37,32,256]{2,1,0:T(8,128)(2,1)}, bf16[37,32,256]{2,1,0:T(8,128)(2,1)}, u32[]{:S(2)}, u32[]{:S(2)}) collective-permute-start(bf16[37,32,256]{2,1,0:T(8,128)(2,1)} %get-tuple-element.22), channel_id=1, source_target_pairs={{0,24},{1,25},{2,26},{3,27},{4,28},{5,29},{6,30},{7,31},{8,16},{9,... | collective-permute-start | bytes 1818632 | tf_op jit(solution)/shard_map/ppermute | solution.py:221
  16.1 47.2 %collective-permute-start.7 = (bf16[37,32,256]{2,1,0:T(8,128)(2,1)}, bf16[37,32,256]{2,1,0:T(8,128)(2,1)}, u32[]{:S(2)}, u32[]{:S(2)}) collective-permute-start(bf16[37,32,256]{2,1,0:T(8,128)(2,1)} %get-tuple-element.23), channel_id=1, source_target_pairs={{0,16},{1,17},{2,18},{3,19},{4,20},{5,21},{6,22},{7,23},{8,24},{9,... | collective-permute-start | bytes 1818632 | tf_op jit(solution)/shard_map/ppermute | solution.py:221
  16.7 48.7 %collective-permute-start.5 = (bf16[37,32,256]{2,1,0:T(8,128)(2,1)}, bf16[37,32,256]{2,1,0:T(8,128)(2,1)}, u32[]{:S(2)}, u32[]{:S(2)}) collective-permute-start(bf16[37,32,256]{2,1,0:T(8,128)(2,1)} %get-tuple-element.21), channel_id=1, source_target_pairs={{0,8},{1,9},{2,10},{3,11},{4,12},{5,13},{6,14},{7,15},{8,0},{9,1},... | collective-permute-start | bytes 1818632 | tf_op jit(solution)/shard_map/ppermute | solution.py:221
  23.5 8.0 %copy-start.8 = (bf16[64,64,3,3]{1,0,3,2:T(8,128)(2,1)S(1)}, bf16[64,64,3,3]{1,0,3,2:T(8,128)(2,1)}, u32[]{:S(2)}) copy-start(bf16[64,64,3,3]{1,0,3,2:T(8,128)(2,1)} %param.10) | copy-start | bytes 221188
  25.5 8.3 %copy-start.14 = (f32[37]{0:T(128)S(1)}, f32[37]{0:T(128)}, u32[]{:S(2)}) copy-start(f32[37]{0:T(128)} %param.13) | copy-start | bytes 448
  25.5 9.0 %copy-start.12 = (s32[1024]{0:T(1024)S(1)}, s32[1024]{0:T(1024)}, u32[]{:S(2)}) copy-start(s32[1024]{0:T(1024)} %param.9) | copy-start | bytes 12292
  38.6 8.0 %collective-permute-start.3 = (bf16[136,64,4]{0,1,2:T(8,128)(2,1)S(1)}, bf16[136,64,4]{0,1,2:T(8,128)(2,1)S(1)}, u32[]{:S(2)}, u32[]{:S(2)}) collective-permute-start(bf16[136,64,4]{0,1,2:T(8,128)(2,1)S(1)} %pad_maximum_fusion.3), channel_id=1, source_target_pairs={{1,0},{2,1},{3,2},{5,4},{6,5},{7,6},{9,8},{10,9},{11,10},{13,12},{... | collective-permute-start | bytes 208904 | tf_op jit(solution)/shard_map/ppermute | solution.py:255
  41.2 10.6 %collective-permute-start.2 = (bf16[136,64,4]{0,1,2:T(8,128)(2,1)S(1)}, bf16[136,64,4]{0,1,2:T(8,128)(2,1)S(1)}, u32[]{:S(2)}, u32[]{:S(2)}) collective-permute-start(bf16[136,64,4]{0,1,2:T(8,128)(2,1)S(1)} %pad_maximum_fusion.2), channel_id=1, source_target_pairs={{0,1},{1,2},{2,3},{4,5},{5,6},{6,7},{8,9},{9,10},{10,11},{12,13},{... | collective-permute-start | bytes 208904 | tf_op jit(solution)/shard_map/ppermute | solution.py:254
  46.6 23.5 %collective-permute-start.4 = (bf16[37,32,128]{2,1,0:T(8,128)(2,1)}, bf16[37,32,128]{2,1,0:T(8,128)(2,1)S(1)}, u32[]{:S(2)}, u32[]{:S(2)}) collective-permute-start(bf16[37,32,128]{2,1,0:T(8,128)(2,1)} %get-tuple-element.25), channel_id=1, source_target_pairs={{0,0},{1,8},{2,16},{3,24},{4,4},{5,12},{6,20},{7,28},{8,1},{9,9},{... | collective-permute-start | bytes 909320 | tf_op jit(solution)/shard_map/ppermute | solution.py:228
  51.8 15.5 %copy-start.15 = (bf16[128]{0:T(256)(128)(2,1)S(1)}, bf16[128]{0:T(256)(128)(2,1)}, u32[]{:S(2)}) copy-start(bf16[128]{0:T(256)(128)(2,1)} %pad.15.clone) | copy-start | bytes 772
  51.8 70.8 %collective-permute-start.11 = (bf16[37,32,128]{2,1,0:T(8,128)(2,1)S(1)}, bf16[37,32,128]{2,1,0:T(8,128)(2,1)S(1)}, u32[]{:S(2)}, u32[]{:S(2)}) collective-permute-start(bf16[37,32,128]{2,1,0:T(8,128)(2,1)S(1)} %get-tuple-element.24), channel_id=1, source_target_pairs={{0,4},{1,12},{2,20},{3,28},{4,0},{5,8},{6,16},{7,24},{8,5},{9,13},... | collective-permute-start | bytes 909320 | tf_op jit(solution)/shard_map/ppermute | solution.py:228
  56.3 11.0 %copy-start.2 = (bf16[136,64,4]{2,1,0:T(8,128)(2,1)S(1)}, bf16[136,64,4]{2,1,0:T(8,128)(2,1)}, u32[]{:S(2)}) copy-start(bf16[136,64,4]{2,1,0:T(8,128)(2,1)} %copy.39) | copy-start | bytes 208900
  57.5 36.0 %collective-permute-start.10 = (bf16[37,32,128]{2,1,0:T(8,128)(2,1)S(1)}, bf16[37,32,128]{2,1,0:T(8,128)(2,1)S(1)}, u32[]{:S(2)}, u32[]{:S(2)}) collective-permute-start(bf16[37,32,128]{2,1,0:T(8,128)(2,1)S(1)} %get-tuple-element.31), channel_id=1, source_target_pairs={{0,3},{1,11},{2,19},{3,27},{4,7},{5,15},{6,23},{7,31},{8,2},{9,10}... | collective-permute-start | bytes 909320 | tf_op jit(solution)/shard_map/ppermute | solution.py:228
  64.5 29.7 %collective-permute-start.8 = (bf16[37,32,128]{2,1,0:T(8,128)(2,1)S(1)}, bf16[37,32,128]{2,1,0:T(8,128)(2,1)S(1)}, u32[]{:S(2)}, u32[]{:S(2)}) collective-permute-start(bf16[37,32,128]{2,1,0:T(8,128)(2,1)S(1)} %get-tuple-element.29), channel_id=1, source_target_pairs={{0,2},{1,10},{2,18},{3,26},{4,6},{5,14},{6,22},{7,30},{8,3},{9,11}... | collective-permute-start | bytes 909320 | tf_op jit(solution)/shard_map/ppermute | solution.py:228
  67.3 54.2 %collective-permute-start.6 = (bf16[37,32,128]{2,1,0:T(8,128)(2,1)}, bf16[37,32,128]{2,1,0:T(8,128)(2,1)}, u32[]{:S(2)}, u32[]{:S(2)}) collective-permute-start(bf16[37,32,128]{2,1,0:T(8,128)(2,1)} %get-tuple-element.27), channel_id=1, source_target_pairs={{0,1},{1,9},{2,17},{3,25},{4,5},{5,13},{6,21},{7,29},{8,0},{9,8},{... | collective-permute-start | bytes 909320 | tf_op jit(solution)/shard_map/ppermute | solution.py:228
  70.1 52.6 %collective-permute-start.14 = (bf16[37,32,128]{2,1,0:T(8,128)(2,1)S(1)}, bf16[37,32,128]{2,1,0:T(8,128)(2,1)S(1)}, u32[]{:S(2)}, u32[]{:S(2)}) collective-permute-start(bf16[37,32,128]{2,1,0:T(8,128)(2,1)S(1)} %get-tuple-element.30), channel_id=1, source_target_pairs={{0,7},{1,15},{2,23},{3,31},{4,3},{5,11},{6,19},{7,27},{8,6},{9,14}... | collective-permute-start | bytes 909320 | tf_op jit(solution)/shard_map/ppermute | solution.py:228
  93.5 29.2 %collective-permute-start.13 = (bf16[37,32,128]{2,1,0:T(8,128)(2,1)S(1)}, bf16[37,32,128]{2,1,0:T(8,128)(2,1)S(1)}, u32[]{:S(2)}, u32[]{:S(2)}) collective-permute-start(bf16[37,32,128]{2,1,0:T(8,128)(2,1)S(1)} %get-tuple-element.28), channel_id=1, source_target_pairs={{0,6},{1,14},{2,22},{3,30},{4,2},{5,10},{6,18},{7,26},{8,7},{9,15}... | collective-permute-start | bytes 909320 | tf_op jit(solution)/shard_map/ppermute | solution.py:228
  94.9 26.6 %copy-start.5 = (bf16[37,32,128]{2,1,0:T(8,128)(2,1)S(1)}, bf16[37,32,128]{2,1,0:T(8,128)(2,1)}, u32[]{:S(2)}) copy-start(bf16[37,32,128]{2,1,0:T(8,128)(2,1)} %copy-done.4) | copy-start | bytes 909316
  94.9 26.6 %copy-start.7 = (bf16[37,32,128]{2,1,0:T(8,128)(2,1)S(1)}, bf16[37,32,128]{2,1,0:T(8,128)(2,1)}, u32[]{:S(2)}) copy-start(bf16[37,32,128]{2,1,0:T(8,128)(2,1)} %copy-done.6) | copy-start | bytes 909316
  94.9 27.7 %collective-permute-start.12 = (bf16[37,32,128]{2,1,0:T(8,128)(2,1)}, bf16[37,32,128]{2,1,0:T(8,128)(2,1)S(1)}, u32[]{:S(2)}, u32[]{:S(2)}) collective-permute-start(bf16[37,32,128]{2,1,0:T(8,128)(2,1)} %get-tuple-element.26), channel_id=1, source_target_pairs={{0,5},{1,13},{2,21},{3,29},{4,1},{5,9},{6,17},{7,25},{8,4},{9,12},... | collective-permute-start | bytes 909320 | tf_op jit(solution)/shard_map/ppermute | solution.py:228
  (7 other events, 29.2 us)

commit v2 on v1

--- a/solution.py
+++ b/solution.py
@@ -204,7 +204,7 @@
         compiler_params=pltpu.CompilerParams(collective_id=0, has_side_effects=True),
     )(x)
 
-def mirrored(teacher):
+def mirrored(teacher, pre):
     bins, rows, cols = teacher.shape
     n_row, n_col = lax.axis_size("row"), lax.axis_size("col")
     k = n_row // n_col
@@ -220,6 +220,7 @@
         if d:
             q = lax.ppermute(q, ("row", "col"), [(at(p, u, z), at(p ^ d, u, z)) for p, u, z in places])
         strips.append(q)
+    strips[2], strips[3], pre = lax.optimization_barrier((strips[2], strips[3], pre))
     for d, q in enumerate(strips):
         for e in range(k):
             half = (core + e) % k
@@ -228,11 +229,10 @@
             got[e][d] = lax.ppermute(piece, ("row", "col"), moves)
     parts = [jnp.concatenate(g, axis=1) for g in got]
     if k == 1:
-        return parts[0]
+        return parts[0], pre
     stacked = jnp.stack(parts)
-    return jnp.concatenate(
-        [lax.dynamic_index_in_dim(stacked, (core - j) % k, 0, False) for j in range(k)], axis=1
-    )
+    ordered = [lax.dynamic_index_in_dim(stacked, (core - j) % k, 0, False) for j in range(k)]
+    return jnp.concatenate(ordered, axis=1), pre
 
 
 def on_device(teacher, features, valid, w_conv, b_conv, w_head, b_head):
@@ -255,7 +255,6 @@
     right = lax.ppermute(edge[:, :, :STEP], "col", [(i + 1, i) for i in range(n_col - 1)])
     side = jnp.concatenate([left, jnp.zeros((rows + 2 * STEP, ch, 128 - 2 * STEP), left.dtype), right], axis=2)
 
-    mirror = mirrored(teacher)
 
     kernel_w = jnp.transpose(w_conv, (0, 2, 3, 1)).reshape(ch, 9 * ch)
     wide, pre = pl.pallas_call(
@@ -273,6 +272,7 @@
         ),
     )(feat, top, bottom, side, kernel_w, b_conv[:, None])
 
+    mirror, pre = mirrored(teacher, pre)
     mirror = jnp.transpose(mirror, (2, 0, 1))
     own = jnp.transpose(teacher, (1, 0, 2))
 

time: 216 us -> 214 us (level)
  Pallas kernels: 102 us -> 79.7 us
  waiting for transfers between devices: 0.04 us -> 18.4 us
  starting transfers between devices: 49.5 us -> 42.2 us
  local copies, waits for them, and re-layouts: 50.1 us -> 54.7 us
  other arithmetic: 9.49 us -> 13.8 us
    pallas_call x1, Pallas kernels: 44.4 us -> 21.8 us  [summed(): pl.pallas_call(functools.partial(sum_kernel, n_row, n_col, chunk), name='...]
    ppermute x1, waiting for transfers between devices: 0.01 us -> 13.6 us  [on_device(): lax.ppermute(edge[:, :, :STEP], 'col', [(i + 1, i) for i in range(n_col -...]
    ppermute x8, starting transfers between devices: 32.7 us -> 25.7 us  [mirrored(): got[e][d] = lax.ppermute(piece, ('row', 'col'), moves)]
    ppermute x8, waiting for transfers between devices: 0.02 us -> 4.8 us  [mirrored(): got[e][d] = lax.ppermute(piece, ('row', 'col'), moves)]
    concatenate x1, other arithmetic: 2.78 us -> 5.03 us  [on_device(): jnp.concatenate([left, jnp.zeros((rows + 2 * STEP, ch, 128 - 2 * STEP), l...]
    unnamed x35 -> x17, local copies, waits for them, and re-layouts: 9.25 us -> 8.28 us
  transfers between devices with their start and end apart: 15 -> 15, of which waited for: 0 -> 2; matrix products, arithmetic and copies ran while one was open for 18% -> 22% of each run, Pallas kernels for 12% -> 12%
where the time goes in v2:
time: 214 us; the launch traced here: 213 us
  Pallas kernels  79.7 us (37%)
  local copies, waits for them, and re-layouts  54.7 us (26%)
  starting transfers between devices  42.2 us (20%)
  waiting for transfers between devices  18.4 us (9%)
  other arithmetic  13.8 us (6%)
  between operations  3.98 us (2%)
    pallas_call x1, Pallas kernels, on_device(): pl.pallas_call(functools.partial(rest_kernel, wave, block, rows, cols, ch...  31.7 us
    pallas_call x1, Pallas kernels, on_device(): pl.pallas_call(functools.partial(conv_kernel, rows, cols, ch), name='conv...  26.1 us
    ppermute x8, starting transfers between devices, mirrored(): got[e][d] = lax.ppermute(piece, ('row', 'col'), moves)  25.7 us
    pallas_call x1, Pallas kernels, summed(): pl.pallas_call(functools.partial(sum_kernel, n_row, n_col, chunk), name='...  21.8 us
    ppermute x1, waiting for transfers between devices, on_device(): lax.ppermute(edge[:, :, :STEP], 'col', [(i + 1, i) for i in range(n_col -...  13.6 us
    unnamed x17, local copies, waits for them, and re-layouts  8.28 us
    slice x2, local copies, waits for them, and re-layouts, on_device(): feat[:, :, -STEP:]  6.77 us
    ppermute x3, starting transfers between devices, mirrored(): lax.ppermute(q, ('row', 'col'), [(at(p, u, z), at(p ^ d, u, z)) for p, u,...  6.62 us
  transfers between devices with their start and end apart: 15, of which 2 were waited for; matrix products, arithmetic and copies ran while one was open for 22% of the time, Pallas kernels for 12%

profile of v2, /device:TPU:0, one launch (start us, length us, event | category | flops | bytes accessed | tf_op | source)
XLA Modules:
  0.0 212.7 jit_solution(10537753589919385416)
XLA Ops:
  0.6 4.7 %copy.52 = bf16[64,128,256]{2,0,1:T(8,128)(2,1)S(1)} copy(bf16[64,128,256]{2,1,0:T(8,128)(2,1)} %param.8) | data formatting | bytes 8388608 | tf_op args[1]
  6.1 3.0 %collective-permute-start.2 = (bf16[4,64,256]{2,1,0:T(8,128)(2,1)}, bf16[4,64,256]{2,1,0:T(8,128)(2,1)}, u32[]{:S(2)}, u32[]{:S(2)}) collective-permute-start(bf16[4,64,256]{2,1,0:T(8,128)(2,1)} %get-tuple-element.23), channel_id=1, source_target_pairs={{0,4},{4,8},{8,12},{12,16},{16,20},{20,24},{24,28},{1,5},{5,9},{9,... | collective-permute-start | bytes 393224 | tf_op jit(solution)/shard_map/ppermute | solution.py:18
  11.7 5.2 %collective-permute-start = (bf16[37,32,256]{2,1,0:T(8,128)(2,1)}, bf16[37,32,256]{2,1,0:T(8,128)(2,1)}, u32[]{:S(2)}, u32[]{:S(2)}) collective-permute-start(bf16[37,32,256]{2,1,0:T(8,128)(2,1)} %get-tuple-element.28), channel_id=1, source_target_pairs={{0,16},{1,17},{2,18},{3,19},{4,20},{5,21},{6,22},{7,23},{8,24},{9,... | collective-permute-start | bytes 1818632 | tf_op jit(solution)/shard_map/ppermute | solution.py:221
  18.3 3.0 %fusion.2 = (bf16[128,64,4]{2,1,0:T(8,128)(2,1)}, bf16[128,64,4]{2,1,0:T(8,128)(2,1)}) fusion(bf16[128,64,256]{2,1,0:T(8,128)(2,1)S(1)} %bitcast.24), kind=kLoop, calls=%fused_computation.26 | loop fusion | bytes 262144 | tf_op jit(solution)/shard_map/slice | solution.py:250
  21.4 3.7 %copy.34 = bf16[128,64,4]{0,1,2:T(8,128)(2,1)S(1)} copy(bf16[128,64,4]{2,1,0:T(8,128)(2,1)} %get-tuple-element.20) | data formatting | bytes 131072 | tf_op jit(solution)/shard_map/slice | solution.py:250
  25.1 3.7 %copy.37 = bf16[128,64,4]{0,1,2:T(8,128)(2,1)S(1)} copy(bf16[128,64,4]{2,1,0:T(8,128)(2,1)} %get-tuple-element.21) | data formatting | bytes 131072 | tf_op jit(solution)/shard_map/slice | solution.py:249
  34.5 4.1 %collective-permute-start.4 = (bf16[136,64,4]{0,1,2:T(8,128)(2,1)}, bf16[136,64,4]{0,1,2:T(8,128)(2,1)}, u32[]{:S(2)}, u32[]{:S(2)}) collective-permute-start(bf16[136,64,4]{0,1,2:T(8,128)(2,1)} %pad_maximum_fusion.2), channel_id=1, source_target_pairs={{0,1},{1,2},{2,3},{4,5},{5,6},{6,7},{8,9},{9,10},{10,11},{12,13},{... | collective-permute-start | bytes 208904 | tf_op jit(solution)/shard_map/ppermute | solution.py:254
  40.6 1.5 collective-permute-start.5
  42.9 5.2 %copy.39 = bf16[136,64,4]{2,1,0:T(8,128)(2,1)} copy(bf16[136,64,4]{0,1,2:T(8,128)(2,1)} %collective-permute-done.4) | data formatting | bytes 139264 | tf_op jit(solution)/shard_map/ppermute | solution.py:254
  48.1 13.6 %collective-permute-done.5 = bf16[136,64,4]{0,1,2:T(8,128)(2,1)S(1)} collective-permute-done((bf16[136,64,4]{0,1,2:T(8,128)(2,1)}, bf16[136,64,4]{0,1,2:T(8,128)(2,1)S(1)}, u32[]{:S(2)}, u32[]{:S(2)}) %collective-permute-start.5) | collective-permute-done | bytes 69664 | tf_op jit(solution)/shard_map/ppermute | solution.py:255
  61.7 4.3 %copy.40 = bf16[136,64,4]{2,1,0:T(8,128)(2,1)} copy(bf16[136,64,4]{0,1,2:T(8,128)(2,1)S(1)} %collective-permute-done.5) | data formatting | bytes 139264 | tf_op jit(solution)/shard_map/ppermute | solution.py:255
  66.0 5.0 %pad_maximum_fusion.side_ref = bf16[136,64,128]{2,1,0:T(8,128)(2,1)} fusion(bf16[136,64,4]{2,1,0:T(8,128)(2,1)} %copy.40, bf16[136,64,4]{2,1,0:T(8,128)(2,1)} %copy.39, bf16[128]{0:T(256)(128)(2,1)S(1)} %pad.15.clone), kind=kLoop, calls=%fused_computation.7 | loop fusion | flops 6684672 | bytes 2367744 | tf_op jit(solution)/shard_map/concatenate | solution.py:256
  71.0 26.1 %conv_forward.1 = (bf16[26112,256]{1,0:T(8,128)(2,1)}, f32[128,64,256]{2,1,0:T(8,128)}) custom-call(bf16[128,64,256]{2,1,0:T(8,128)(2,1)} %bitcast.25, bf16[4,64,256]{2,1,0:T(8,128)(2,1)} %collective-permute-done.2.top_ref, bf16[4,64,256]{2,1,0:T(8,128)(2,1)} %collective-permute-done.3.bottom_ref, bf16[136,64,128]{2,1,0:T(8,128)(2,1)} %pad_maximum_fusion.side_ref, ...), custom_call_target="tpu_custom_call" | custom-call | flops 2415919104 | bytes 30000000 | tf_op jit(solution)/shard_map/conv_forward/pallas_call | solution.py:260
  98.3 1.8 constant_dynamic-slice_fusion
  100.1 1.9 constant_dynamic-slice_fusion.2
  103.4 4.8 %collective-permute-done.13 = bf16[37,32,128]{2,1,0:T(8,128)(2,1)} collective-permute-done((bf16[37,32,128]{2,1,0:T(8,128)(2,1)S(1)}, bf16[37,32,128]{2,1,0:T(8,128)(2,1)}, u32[]{:S(2)}, u32[]{:S(2)}) %collective-permute-start.13) | collective-permute-done | bytes 303136 | tf_op jit(solution)/shard_map/ppermute | solution.py:229
  108.2 2.3 %collective-permute-start.10 = (bf16[37,32,128]{2,1,0:T(8,128)(2,1)}, bf16[37,32,128]{2,1,0:T(8,128)(2,1)}, u32[]{:S(2)}, u32[]{:S(2)}) collective-permute-start(bf16[37,32,128]{2,1,0:T(8,128)(2,1)} %get-tuple-element.37), channel_id=1, source_target_pairs={{0,3},{1,11},{2,19},{3,27},{4,7},{5,15},{6,23},{7,31},{8,2},{9,10}... | collective-permute-start | bytes 909320 | tf_op jit(solution)/shard_map/ppermute | solution.py:229
  110.5 22.0 %collective-permute-start.8 = (bf16[37,32,128]{2,1,0:T(8,128)(2,1)}, bf16[37,32,128]{2,1,0:T(8,128)(2,1)}, u32[]{:S(2)}, u32[]{:S(2)}) collective-permute-start(bf16[37,32,128]{2,1,0:T(8,128)(2,1)} %get-tuple-element.33), channel_id=1, source_target_pairs={{0,1},{1,9},{2,17},{3,25},{4,5},{5,13},{6,21},{7,29},{8,0},{9,8},{... | collective-permute-start | bytes 909320 | tf_op jit(solution)/shard_map/ppermute | solution.py:229
  132.5 2.9 %copy.53 = bf16[37,128,256]{2,0,1:T(8,128)(2,1)} copy(bf16[37,128,256]{2,1,0:T(8,128)(2,1)S(1)} %copy-done.1) | data formatting | bytes 4849664 | tf_op args[0]
  142.6 2.0 fusion.1
  145.9 2.1 %copy.46 = bf16[1,37,128,128]{2,1,3,0:T(8,128)(2,1)S(1)} copy(bf16[1,37,128,128]{3,2,1,0:T(8,128)(2,1)} %get-tuple-element.25) | data formatting | bytes 2424832 | tf_op jit(solution)/shard_map/jit(dynamic_index_in_dim)/dynamic_slice | solution.py:234
  148.1 1.9 maximum_bitcast_fusion.mirror_ref
  150.0 31.7 %loss_and_grads.1 = (f32[128,256]{1,0:T(8,128)}, f32[448,128]{1,0:T(8,128)}) custom-call(f32[128]{0:T(128)} %dynamic_slice.37.rv_ref, f32[1,256]{1,0:T(1,128)} %bitcast.34, f32[128,64,256]{2,1,0:T(8,128)} %get-tuple-element.14.pre_ref, bf16[128,37,256]{2,1,0:T(8,128)(2,1)} %bitcast.26, bf16[128,37,256]{2,1,0:T(8,128)(2,1)} %maximum_bitcast_fusion.mirror_ref, ...), custom_call_target="tpu_custom_call" | custom-call | tf_op jit(solution)/shard_map/loss_and_grads/pallas_call | solution.py:289
  181.7 21.8 %sum_over_devices.1 = f32[448,128]{1,0:T(8,128)} custom-call(f32[448,128]{1,0:T(8,128)} %get-tuple-element.19.x_ref), custom_call_target="tpu_custom_call" | custom-call | tf_op jit(solution)/shard_map/sum_over_devices/pallas_call | solution.py:189
  (69 shorter events, 30.3 us)
Async XLA Ops:
  0.6 9.8 %copy-start.1 = (bf16[37,128,256]{2,1,0:T(8,128)(2,1)S(1)}, bf16[37,128,256]{2,1,0:T(8,128)(2,1)}, u32[]{:S(2)}) copy-start(bf16[37,128,256]{2,1,0:T(8,128)(2,1)} %param.7) | copy-start | bytes 7274500
  5.4 13.0 %copy-start = (bf16[64,128,256]{2,0,1:T(8,128)(2,1)}, bf16[64,128,256]{2,0,1:T(8,128)(2,1)S(1)}, u32[]{:S(2)}) copy-start(bf16[64,128,256]{2,0,1:T(8,128)(2,1)S(1)} %copy.52) | copy-start | bytes 12582916
  6.1 24.4 %collective-permute-start.2 = (bf16[4,64,256]{2,1,0:T(8,128)(2,1)}, bf16[4,64,256]{2,1,0:T(8,128)(2,1)}, u32[]{:S(2)}, u32[]{:S(2)}) collective-permute-start(bf16[4,64,256]{2,1,0:T(8,128)(2,1)} %get-tuple-element.23), channel_id=1, source_target_pairs={{0,4},{4,8},{8,12},{12,16},{16,20},{20,24},{24,28},{1,5},{5,9},{9,... | collective-permute-start | bytes 393224 | tf_op jit(solution)/shard_map/ppermute | solution.py:18
  9.1 23.0 %collective-permute-start.3 = (bf16[4,64,256]{2,1,0:T(8,128)(2,1)}, bf16[4,64,256]{2,1,0:T(8,128)(2,1)}, u32[]{:S(2)}, u32[]{:S(2)}) collective-permute-start(bf16[4,64,256]{2,1,0:T(8,128)(2,1)} %get-tuple-element.22), channel_id=1, source_target_pairs={{4,0},{8,4},{12,8},{16,12},{20,16},{24,20},{28,24},{5,1},{9,5},{13... | collective-permute-start | bytes 393224 | tf_op jit(solution)/shard_map/ppermute | solution.py:19
  11.7 85.4 %collective-permute-start = (bf16[37,32,256]{2,1,0:T(8,128)(2,1)}, bf16[37,32,256]{2,1,0:T(8,128)(2,1)}, u32[]{:S(2)}, u32[]{:S(2)}) collective-permute-start(bf16[37,32,256]{2,1,0:T(8,128)(2,1)} %get-tuple-element.28), channel_id=1, source_target_pairs={{0,16},{1,17},{2,18},{3,19},{4,20},{5,21},{6,22},{7,23},{8,24},{9,... | collective-permute-start | bytes 1818632 | tf_op jit(solution)/shard_map/ppermute | solution.py:221
  16.9 80.2 %collective-permute-start.1 = (bf16[37,32,256]{2,1,0:T(8,128)(2,1)}, bf16[37,32,256]{2,1,0:T(8,128)(2,1)}, u32[]{:S(2)}, u32[]{:S(2)}) collective-permute-start(bf16[37,32,256]{2,1,0:T(8,128)(2,1)} %get-tuple-element.27), channel_id=1, source_target_pairs={{0,24},{1,25},{2,26},{3,27},{4,28},{5,29},{6,30},{7,31},{8,16},{9,... | collective-permute-start | bytes 1818632 | tf_op jit(solution)/shard_map/ppermute | solution.py:221
  17.4 82.7 %collective-permute-start.7 = (bf16[37,32,256]{2,1,0:T(8,128)(2,1)}, bf16[37,32,256]{2,1,0:T(8,128)(2,1)}, u32[]{:S(2)}, u32[]{:S(2)}) collective-permute-start(bf16[37,32,256]{2,1,0:T(8,128)(2,1)} %get-tuple-element.29), channel_id=1, source_target_pairs={{0,8},{1,9},{2,10},{3,11},{4,12},{5,13},{6,14},{7,15},{8,0},{9,1},... | collective-permute-start | bytes 1818632 | tf_op jit(solution)/shard_map/ppermute | solution.py:221
  21.4 7.5 %copy-start.2 = (bf16[64,64,3,3]{1,0,3,2:T(8,128)(2,1)S(1)}, bf16[64,64,3,3]{1,0,3,2:T(8,128)(2,1)}, u32[]{:S(2)}) copy-start(bf16[64,64,3,3]{1,0,3,2:T(8,128)(2,1)} %param.10) | copy-start | bytes 221188
  21.4 8.4 %copy-start.5 = (f32[64]{0:T(128)S(1)}, f32[64]{0:T(128)}, u32[]{:S(2)}) copy-start(f32[64]{0:T(128)} %param.11) | copy-start | bytes 772
  34.5 8.4 %collective-permute-start.4 = (bf16[136,64,4]{0,1,2:T(8,128)(2,1)}, bf16[136,64,4]{0,1,2:T(8,128)(2,1)}, u32[]{:S(2)}, u32[]{:S(2)}) collective-permute-start(bf16[136,64,4]{0,1,2:T(8,128)(2,1)} %pad_maximum_fusion.2), channel_id=1, source_target_pairs={{0,1},{1,2},{2,3},{4,5},{5,6},{6,7},{8,9},{9,10},{10,11},{12,13},{... | collective-permute-start | bytes 208904 | tf_op jit(solution)/shard_map/ppermute | solution.py:254
  40.6 21.1 %collective-permute-start.5 = (bf16[136,64,4]{0,1,2:T(8,128)(2,1)}, bf16[136,64,4]{0,1,2:T(8,128)(2,1)S(1)}, u32[]{:S(2)}, u32[]{:S(2)}) collective-permute-start(bf16[136,64,4]{0,1,2:T(8,128)(2,1)} %pad_maximum_fusion.3), channel_id=1, source_target_pairs={{1,0},{2,1},{3,2},{5,4},{6,5},{7,6},{9,8},{10,9},{11,10},{13,12},{... | collective-permute-start | bytes 208904 | tf_op jit(solution)/shard_map/ppermute | solution.py:255
  42.9 60.5 %collective-permute-start.11 = (bf16[37,32,128]{2,1,0:T(8,128)(2,1)}, bf16[37,32,128]{2,1,0:T(8,128)(2,1)S(1)}, u32[]{:S(2)}, u32[]{:S(2)}) collective-permute-start(bf16[37,32,128]{2,1,0:T(8,128)(2,1)} %get-tuple-element.30), channel_id=1, source_target_pairs={{0,4},{1,12},{2,20},{3,28},{4,0},{5,8},{6,16},{7,24},{8,5},{9,13},... | collective-permute-start | bytes 909320 | tf_op jit(solution)/shard_map/ppermute | solution.py:229
  98.2 10.0 %collective-permute-start.13 = (bf16[37,32,128]{2,1,0:T(8,128)(2,1)S(1)}, bf16[37,32,128]{2,1,0:T(8,128)(2,1)}, u32[]{:S(2)}, u32[]{:S(2)}) collective-permute-start(bf16[37,32,128]{2,1,0:T(8,128)(2,1)S(1)} %get-tuple-element.34), channel_id=1, source_target_pairs={{0,6},{1,14},{2,22},{3,30},{4,2},{5,10},{6,18},{7,26},{8,7},{9,15}... | collective-permute-start | bytes 909320 | tf_op jit(solution)/shard_map/ppermute | solution.py:229
  100.1 10.4 %collective-permute-start.14 = (bf16[37,32,128]{2,1,0:T(8,128)(2,1)S(1)}, bf16[37,32,128]{2,1,0:T(8,128)(2,1)}, u32[]{:S(2)}, u32[]{:S(2)}) collective-permute-start(bf16[37,32,128]{2,1,0:T(8,128)(2,1)S(1)} %get-tuple-element.36), channel_id=1, source_target_pairs={{0,7},{1,15},{2,23},{3,31},{4,3},{5,11},{6,19},{7,27},{8,6},{9,14}... | collective-permute-start | bytes 909320 | tf_op jit(solution)/shard_map/ppermute | solution.py:229
  102.0 37.8 %collective-permute-start.12 = (bf16[37,32,128]{2,1,0:T(8,128)(2,1)}, bf16[37,32,128]{2,1,0:T(8,128)(2,1)}, u32[]{:S(2)}, u32[]{:S(2)}) collective-permute-start(bf16[37,32,128]{2,1,0:T(8,128)(2,1)} %get-tuple-element.32), channel_id=1, source_target_pairs={{0,5},{1,13},{2,21},{3,29},{4,1},{5,9},{6,17},{7,25},{8,4},{9,12},... | collective-permute-start | bytes 909320 | tf_op jit(solution)/shard_map/ppermute | solution.py:229
  102.0 39.1 %collective-permute-start.6 = (bf16[37,32,128]{2,1,0:T(8,128)(2,1)S(1)}, bf16[37,32,128]{2,1,0:T(8,128)(2,1)}, u32[]{:S(2)}, u32[]{:S(2)}) collective-permute-start(bf16[37,32,128]{2,1,0:T(8,128)(2,1)S(1)} %get-tuple-element.31), channel_id=1, source_target_pairs={{0,0},{1,8},{2,16},{3,24},{4,4},{5,12},{6,20},{7,28},{8,1},{9,9},{... | collective-permute-start | bytes 909320 | tf_op jit(solution)/shard_map/ppermute | solution.py:229
  103.4 37.7 %collective-permute-start.9 = (bf16[37,32,128]{2,1,0:T(8,128)(2,1)S(1)}, bf16[37,32,128]{2,1,0:T(8,128)(2,1)}, u32[]{:S(2)}, u32[]{:S(2)}) collective-permute-start(bf16[37,32,128]{2,1,0:T(8,128)(2,1)S(1)} %get-tuple-element.35), channel_id=1, source_target_pairs={{0,2},{1,10},{2,18},{3,26},{4,6},{5,14},{6,22},{7,30},{8,3},{9,11}... | collective-permute-start | bytes 909320 | tf_op jit(solution)/shard_map/ppermute | solution.py:229
  108.2 33.0 %collective-permute-start.10 = (bf16[37,32,128]{2,1,0:T(8,128)(2,1)}, bf16[37,32,128]{2,1,0:T(8,128)(2,1)}, u32[]{:S(2)}, u32[]{:S(2)}) collective-permute-start(bf16[37,32,128]{2,1,0:T(8,128)(2,1)} %get-tuple-element.37), channel_id=1, source_target_pairs={{0,3},{1,11},{2,19},{3,27},{4,7},{5,15},{6,23},{7,31},{8,2},{9,10}... | collective-permute-start | bytes 909320 | tf_op jit(solution)/shard_map/ppermute | solution.py:229
  110.5 30.7 %collective-permute-start.8 = (bf16[37,32,128]{2,1,0:T(8,128)(2,1)}, bf16[37,32,128]{2,1,0:T(8,128)(2,1)}, u32[]{:S(2)}, u32[]{:S(2)}) collective-permute-start(bf16[37,32,128]{2,1,0:T(8,128)(2,1)} %get-tuple-element.33), channel_id=1, source_target_pairs={{0,1},{1,9},{2,17},{3,25},{4,5},{5,13},{6,21},{7,29},{8,0},{9,8},{... | collective-permute-start | bytes 909320 | tf_op jit(solution)/shard_map/ppermute | solution.py:229
  132.5 2.9 %copy-start.4 = (s32[1024]{0:T(1024)S(1)}, s32[1024]{0:T(1024)}, u32[]{:S(2)}) copy-start(s32[1024]{0:T(1024)} %param.9) | copy-start | bytes 12292
  132.5 4.1 %copy-start.6 = (f32[37]{0:T(128)S(1)}, f32[37]{0:T(128)}, u32[]{:S(2)}) copy-start(f32[37]{0:T(128)} %param.13) | copy-start | bytes 448
  132.5 4.8 %copy-start.3 = (bf16[37,64]{1,0:T(8,128)(2,1)S(1)}, bf16[37,64]{1,0:T(8,128)(2,1)}, u32[]{:S(2)}) copy-start(bf16[37,64]{1,0:T(8,128)(2,1)} %wh_ref.1) | copy-start | bytes 14212
